TPU v7x, 32 devices: a whole 2x2x4 slice. The times are simulated.
32 devices in a mesh: node: 4 (over z), dom: 8 (over y, x, core).
Axes of the slice: x: 2, y: 2, z: 4, core: 2. Of those that a mesh axis runs over, the one named last changes fastest.
Arguments:
- probes: float32 [32, 16, 16, 128], P(None, 'dom'), may hold values from -24 to 24
- slope: float32 [16, 16, 128], P('dom'), may hold values from 4 to 6
- root: float32 [16, 16, 128], P('dom'), may hold values from 0.3 to 0.7
- damping: float32 [16, 16, 128], P('dom'), may hold values from 0.3 to 1.2
Outputs:
- moments: float32 [2, 2, 32, 16, 16, 128], P(None, None, 'node', 'dom')
- projections: float32 [2, 2, 32, 32], replicated
All inputs are finite; a program needn't handle non-finite values.
Results may differ from a plain program's by a relative error of at most 0.00013.
Values sent between devices are 32-bit elements; how exact they have to be, the bound alone decides.
A program may use at most 64 MiB of HBM per device.

v0:
```python
import math

import jax
import jax.numpy as jnp
from jax import lax
from jax.sharding import PartitionSpec as P

NODE_DEV = 2
SWEEPS = 8


CENTRE = 0.5
RADIUS = 2.0


def grid_step(source, fields, factor_re, factor_im):
    padded = jnp.pad(fields, ((0, 0), (0, 0), (1, 1), (1, 1), (1, 1)))
    total = padded[:, :, 2:, 1:-1, 1:-1] + padded[:, :, :-2, 1:-1, 1:-1]
    total = total + padded[:, :, 1:-1, 2:, 1:-1] + padded[:, :, 1:-1, :-2, 1:-1]
    total = total + padded[:, :, 1:-1, 1:-1, 2:] + padded[:, :, 1:-1, 1:-1, :-2]
    real_part = source + total[:, 0]
    imag_part = total[:, 1]
    return jnp.stack(
        [
            real_part * factor_re - imag_part * factor_im,
            real_part * factor_im + imag_part * factor_re,
        ],
        axis=1,
    )


def inverse_diagonal(shift_real, shift_imaginary, slope, root, damping, guard):
    zr_col = shift_real[:, None, None, None, None]
    zi_col = shift_imaginary[:, None, None, None, None]
    decay = jnp.exp(-zr_col)
    real_d = slope * (zr_col - root) + damping * (decay * jnp.cos(zi_col))
    imag_d = slope * zi_col - damping * (decay * jnp.sin(zi_col))
    scale = 1.0 / (real_d * real_d + imag_d * imag_d + guard)
    return (real_d * scale, -imag_d * scale)


def per_system(fields, weight_re, weight_im):
    a_col = weight_re[:, None, None, None]
    b_col = weight_im[:, None, None, None]
    return jnp.stack(
        [a_col * fields[:, 0] - b_col * fields[:, 1], a_col * fields[:, 1] + b_col * fields[:, 0]]
    )


def body(probes, slope, root, damping):
    vectors = probes.shape[0]
    planes = probes.shape[1]
    groups = lax.axis_size("node")
    total = NODE_DEV * groups
    first = (lax.axis_index("node") * NODE_DEV).astype(jnp.float32)
    dom_size = lax.axis_size("dom")
    count = NODE_DEV * vectors // dom_size
    replicated = jnp.broadcast_to(probes[None], (NODE_DEV,) + probes.shape).reshape(
        (NODE_DEV * vectors,) + probes.shape[1:]
    )
    own = lax.all_to_all(replicated, "dom", split_axis=0, concat_axis=1, tiled=True)
    slope_all, root_all, damping_all = (
        lax.all_gather(slope, "dom", axis=0, tiled=True),
        lax.all_gather(root, "dom", axis=0, tiled=True),
        lax.all_gather(damping, "dom", axis=0, tiled=True),
    )
    system = lax.axis_index("dom") * count + jnp.arange(count)
    position = first + (system // vectors).astype(jnp.float32)
    theta = 2.0 * math.pi * (position + 0.5) / total
    shift_real = CENTRE + RADIUS * jnp.cos(theta)
    shift_imaginary = RADIUS * jnp.sin(theta)
    qre, qim = inverse_diagonal(
        shift_real, shift_imaginary, slope_all[None], root_all[None], damping_all[None], 0.0
    )
    qre = qre[:, 0]
    qim = qim[:, 0]
    fields = jnp.stack([own * qre, own * qim], axis=1)
    for sweep in range(SWEEPS):
        fields = grid_step(own, fields, qre, qim)
    weight_re = RADIUS * jnp.cos(theta) / total
    weight_im = RADIUS * jnp.sin(theta) / total
    shifted_re = weight_re * shift_real - weight_im * shift_imaginary
    shifted_im = weight_re * shift_imaginary + weight_im * shift_real
    terms = jnp.stack(
        [per_system(fields, weight_re, weight_im), per_system(fields, shifted_re, shifted_im)]
    )
    back = lax.all_to_all(terms, "dom", split_axis=3, concat_axis=2, tiled=True)
    local = jnp.sum(back.reshape((2, 2, NODE_DEV, vectors) + probes.shape[1:]), axis=2)
    flat = local.reshape(4 * vectors, -1)
    basis = probes.reshape(vectors, -1)
    partial_value = lax.dot_general(
        flat,
        basis,
        (((1,), (1,)), ((), ())),
        precision=lax.Precision.HIGHEST,
        preferred_element_type=jnp.float32,
    )
    cells = planes * probes.shape[2] * probes.shape[3] * lax.axis_size("dom")
    projections = lax.psum(partial_value.reshape(2, 2, vectors, vectors) / cells, ("node", "dom"))
    summed = lax.psum(local, "node")
    share = vectors // groups
    moments = lax.dynamic_slice_in_dim(summed, lax.axis_index("node") * share, share, 2)
    return (moments, projections)


def solution(mesh):
    in_specs = (
        P(None, "dom", None, None),
        P("dom", None, None),
        P("dom", None, None),
        P("dom", None, None),
    )
    out_specs = (P(None, None, "node", "dom", None, None), P())
    return jax.shard_map(body, mesh=mesh, in_specs=in_specs, out_specs=out_specs, check_vma=False)
```

profile of v0, /device:TPU:0, one launch (start us, length us, event | category | flops | bytes accessed | tf_op | source)
XLA Modules:
  0.0 260.8 jit_solution(6893673430703613702)
XLA Ops:
  7.2 2.2 broadcast_in_dim.2
  9.4 5.2 %all-to-all-start = ((f32[64,2,16,128]{3,2,1,0:T(8,128)}), f32[64,2,16,128]{3,2,1,0:T(8,128)S(1)}, u32[]{:S(2)}, u32[]{:S(2)}) async-start(f32[64,2,16,128]{3,2,1,0:T(8,128)} %bitcast), calls=%async_computation | async-start | bytes 2097152 | tf_op jit(solution)/shard_map/all_to_all | solution.py:61
  14.6 18.8 %all_gather.9 = f32[16,16,128]{2,1,0:T(8,128)S(1)} all-gather(f32[2,16,128]{2,1,0:T(8,128)S(1)} %copy-done.2), channel_id=1, replica_groups=mesh['node'=4,'dom'=8] {'dom'}, dimensions={0}, use_global_device_ids=true | all-gather | bytes 147456 | tf_op jit(solution)/shard_map/all_gather | solution.py:63
  33.4 8.3 %all_gather.10 = f32[16,16,128]{2,1,0:T(8,128)S(1)} all-gather(f32[2,16,128]{2,1,0:T(8,128)S(1)} %copy-done.3), channel_id=1, replica_groups=mesh['node'=4,'dom'=8] {'dom'}, dimensions={0}, use_global_device_ids=true | all-gather | bytes 147456 | tf_op jit(solution)/shard_map/all_gather | solution.py:64
  41.7 9.1 %all_gather.11 = f32[16,16,128]{2,1,0:T(8,128)S(1)} all-gather(f32[2,16,128]{2,1,0:T(8,128)S(1)} %copy-done.4), channel_id=1, replica_groups=mesh['node'=4,'dom'=8] {'dom'}, dimensions={0}, use_global_device_ids=true | all-gather | bytes 147456 | tf_op jit(solution)/shard_map/all_gather | solution.py:65
  50.8 0.1 multiply_subtract_fusion.12
  50.9 0.0 all-to-all-done
  50.9 0.1 copy.15
  51.0 0.6 fusion.19
  51.6 2.6 select_maximum_fusion.7
  54.2 3.3 %slice_add_fusion.35 = f32[8,2,16,16,128]{4,3,2,0,1:T(8,128)S(1)} fusion(f32[8,2,18,18,130]{4,3,2,0,1:T(8,128)S(1)} %select_maximum_fusion.7), kind=kLoop, calls=%fused_computation.56 | loop fusion | flops 2621440 | bytes 14680064 | tf_op jit(solution)/shard_map/add | solution.py:20
  57.5 0.8 multiply_subtract_fusion.10
  58.3 2.4 select_maximum_fusion.6
  60.7 3.3 %slice_add_fusion.30 = f32[8,2,16,16,128]{4,3,2,0,1:T(8,128)S(1)} fusion(f32[8,2,18,18,130]{4,3,2,0,1:T(8,128)S(1)} %select_maximum_fusion.6), kind=kLoop, calls=%fused_computation.51 | loop fusion | flops 2621440 | bytes 14680064 | tf_op jit(solution)/shard_map/add | solution.py:20
  63.9 0.8 multiply_subtract_fusion.9
  64.7 2.4 select_maximum_fusion.5
  67.1 3.3 %slice_add_fusion.25 = f32[8,2,16,16,128]{4,3,2,0,1:T(8,128)S(1)} fusion(f32[8,2,18,18,130]{4,3,2,0,1:T(8,128)S(1)} %select_maximum_fusion.5), kind=kLoop, calls=%fused_computation.46 | loop fusion | flops 2621440 | bytes 14680064 | tf_op jit(solution)/shard_map/add | solution.py:20
  70.4 0.8 multiply_subtract_fusion.8
  71.2 2.4 select_maximum_fusion.4
  73.6 3.3 %slice_add_fusion.20 = f32[8,2,16,16,128]{4,3,2,0,1:T(8,128)S(1)} fusion(f32[8,2,18,18,130]{4,3,2,0,1:T(8,128)S(1)} %select_maximum_fusion.4), kind=kLoop, calls=%fused_computation.41 | loop fusion | flops 2621440 | bytes 14680064 | tf_op jit(solution)/shard_map/add | solution.py:20
  76.8 0.8 multiply_subtract_fusion.7
  77.6 2.6 select_maximum_fusion.3
  80.2 3.3 %slice_add_fusion.15 = f32[8,2,16,16,128]{4,3,2,0,1:T(8,128)S(1)} fusion(f32[8,2,18,18,130]{4,3,2,0,1:T(8,128)S(1)} %select_maximum_fusion.3), kind=kLoop, calls=%fused_computation.36 | loop fusion | flops 2621440 | bytes 14680064 | tf_op jit(solution)/shard_map/add | solution.py:20
  83.5 0.8 multiply_subtract_fusion.6
  84.3 2.4 select_maximum_fusion.2
  86.7 3.3 %slice_add_fusion.10 = f32[8,2,16,16,128]{4,3,2,0,1:T(8,128)S(1)} fusion(f32[8,2,18,18,130]{4,3,2,0,1:T(8,128)S(1)} %select_maximum_fusion.2), kind=kLoop, calls=%fused_computation.31 | loop fusion | flops 2621440 | bytes 14680064 | tf_op jit(solution)/shard_map/add | solution.py:20
  90.0 0.8 multiply_subtract_fusion.5
  90.8 2.4 select_maximum_fusion.1
  93.1 3.3 %slice_add_fusion.5 = f32[8,2,16,16,128]{4,3,2,0,1:T(8,128)S(1)} fusion(f32[8,2,18,18,130]{4,3,2,0,1:T(8,128)S(1)} %select_maximum_fusion.1), kind=kLoop, calls=%fused_computation.26 | loop fusion | flops 2621440 | bytes 14680064 | tf_op jit(solution)/shard_map/add | solution.py:20
  96.4 0.8 multiply_subtract_fusion.4
  97.2 2.4 select_maximum_fusion
  99.6 3.5 %slice_add_fusion = f32[8,2,16,16,128]{4,3,2,0,1:T(8,128)S(1)} fusion(f32[8,2,18,18,130]{4,3,2,0,1:T(8,128)S(1)} %select_maximum_fusion), kind=kLoop, calls=%fused_computation.21 | loop fusion | flops 2621440 | bytes 14680064 | tf_op jit(solution)/shard_map/add | solution.py:20
  103.1 0.9 multiply_subtract_fusion.1
  104.1 0.5 multiply_subtract_fusion
  104.6 0.4 maximum_bitcast_fusion
  105.0 0.4 pad_maximum_fusion
  105.4 0.6 copy.17
  106.0 51.6 %all_to_all.36 = f32[2,2,8,16,16,128]{5,4,2,1,0,3:T(8,128)S(1)} all-to-all(f32[2,2,8,16,16,128]{5,4,2,1,0,3:T(8,128)S(1)} %copy.17), channel_id=1, replica_groups=mesh['node'=4,'dom'=8] {'dom'}, dimensions={3} | all-to-all | bytes 8388608 | tf_op jit(solution)/shard_map/all_to_all | solution.py:87
  157.6 0.5 copy.19
  158.2 0.0 copy-start.1
  158.2 0.5 bitcast_reduce_fusion
  158.7 0.5 copy-done.1
  159.2 3.1 %fusion.10 = f32[2,2,32,32]{3,2,1,0:T(8,128)S(1)} fusion(f32[2,2,32,2,16,128]{5,4,3,2,1,0:T(8,128)S(1)} %bitcast_reduce_fusion, f32[32,2,16,128,1,1]{3,2,1,0,5,4:T(8,128)S(1)} %bitcast.53), kind=kOutput, calls=%fused_computation.66 | convolution fusion | flops 201330688 | bytes 2637824 | tf_op jit(solution)/shard_map/dot_general | solution.py:91
  162.3 0.0 all-reduce.10.cloned.1.call-start
  162.4 0.7 all-reduce.10.cloned.1.call-update
  163.1 42.9 %psum.15 = f32[2,2,32,32]{3,2,1,0:T(8,128)} all-reduce(f32[2,2,32,32]{3,2,1,0:T(8,128)S(1)} %fusion.10), channel_id=1, replica_groups=mesh['node'=4,'dom'=8] {'node','dom'}, use_global_device_ids=true, to_apply=%region_2.3 | all-reduce | flops 4096 | bytes 32768 | tf_op jit(solution)/shard_map/psum | solution.py:99
  206.0 46.1 %all-reduce.10.cloned.1.call-done = f32[2,2,32,2,16,128]{5,4,3,2,1,0:T(8,128)} async-done(((f32[2,2,32,2,16,128]{5,4,3,2,1,0:T(8,128)}), f32[2,2,32,2,16,128]{5,4,3,2,1,0:T(8,128)}) %all-reduce.10.cloned.1.call-update) | async-done | bytes 2097168 | tf_op jit(solution)/shard_map/psum | solution.py:100
  252.1 1.9 constant_dynamic-slice_fusion
  (9 shorter events, 0.1 us)
Async XLA Ops:
  7.2 7.4 %copy-start.2 = (f32[2,16,128]{2,1,0:T(8,128)S(1)}, f32[2,16,128]{2,1,0:T(8,128)}, u32[]{:S(2)}) copy-start(f32[2,16,128]{2,1,0:T(8,128)} %param.5) | copy-start | bytes 49156
  7.2 26.2 %copy-start.3 = (f32[2,16,128]{2,1,0:T(8,128)S(1)}, f32[2,16,128]{2,1,0:T(8,128)}, u32[]{:S(2)}) copy-start(f32[2,16,128]{2,1,0:T(8,128)} %param.6) | copy-start | bytes 49156
  7.2 34.5 %copy-start.4 = (f32[2,16,128]{2,1,0:T(8,128)S(1)}, f32[2,16,128]{2,1,0:T(8,128)}, u32[]{:S(2)}) copy-start(f32[2,16,128]{2,1,0:T(8,128)} %param.7) | copy-start | bytes 49156
  9.4 41.5 %all-to-all-start = ((f32[64,2,16,128]{3,2,1,0:T(8,128)}), f32[64,2,16,128]{3,2,1,0:T(8,128)S(1)}, u32[]{:S(2)}, u32[]{:S(2)}) async-start(f32[64,2,16,128]{3,2,1,0:T(8,128)} %bitcast), calls=%async_computation | async-start | bytes 2097152 | tf_op jit(solution)/shard_map/all_to_all | solution.py:61
  158.2 1.0 copy-start.1
  158.7 3.6 %copy-start = (f32[2,2,32,2,16,128]{5,4,3,2,1,0:T(8,128)}, f32[2,2,32,2,16,128]{5,4,3,2,1,0:T(8,128)S(1)}, u32[]{:S(2)}) copy-start(f32[2,2,32,2,16,128]{5,4,3,2,1,0:T(8,128)S(1)} %bitcast_reduce_fusion) | copy-start | bytes 6291460
  162.3 89.8 %all-reduce.10.cloned.1.call-start = ((), (), s32[]{:S(2)}) async-start(), calls=%async_computation.2 | async-start | bytes 4194304 | tf_op jit(solution)/shard_map/psum | solution.py:100
Sparse Core Ops, SparseCore 0:
  165.5 86.5 all-reduce.9
where the time goes:
time: 261 us
  blocking collectives  131 us (50%)
  other arithmetic  54.8 us (21%)
  waiting for transfers between devices  46.8 us (18%)
  between operations  14.3 us (5%)
  local copies, waits for them, and re-layouts  5.8 us (2%)
  starting transfers between devices  5.24 us (2%)
  matrix products  3.08 us (1%)
    all_to_all x1, blocking collectives, body(): back = lax.all_to_all(terms, 'dom', split_axis=3, concat_axis=2, tiled=True)  51.6 us
    psum x1, waiting for transfers between devices, body(): summed = lax.psum(local, 'node')  46.1 us
    psum x1, blocking collectives, body(): lax.psum(partial_value.reshape(2, 2, vectors, vectors) / cells, ('node',...  42.9 us
    add x8, other arithmetic, grid_step(): total = total + padded[:, :, 1:-1, 1:-1, 2:] + padded[:, :, 1:-1, 1:-1, :-2]  26.4 us
    all_gather x1, blocking collectives, body(): lax.all_gather(slope, 'dom', axis=0, tiled=True)  18.8 us
    another operation x7, other arithmetic, grid_step(): jnp.stack([real_part * factor_re - imag_part * factor_im, real_part * fac...  16.9 us
    all_gather x1, blocking collectives, body(): lax.all_gather(damping, 'dom', axis=0, tiled=True)  9.1 us
    all_gather x1, blocking collectives, body(): lax.all_gather(root, 'dom', axis=0, tiled=True)  8.31 us
  transfers between devices with their start and end apart: 2, of which 1 were waited for; matrix products, arithmetic and copies ran while one was open for 0% of the time, Pallas kernels for 0%

commit v1 on v0

--- a/solution.py
+++ b/solution.py
@@ -1,12 +1,16 @@
+import functools
 import math
 
 import jax
 import jax.numpy as jnp
 from jax import lax
+from jax.experimental import pallas as pl
+from jax.experimental.pallas import tpu as pltpu
 from jax.sharding import PartitionSpec as P
 
 NODE_DEV = 2
 SWEEPS = 8
+UNROLL = 2
 
 
 CENTRE = 0.5
@@ -103,7 +107,364 @@
     return (moments, projections)
 
 
+MESH = pl.DeviceIdType.MESH
+
+
+def contour(total):
+    nodes = []
+    for node in range(total // 2):
+        theta = 2.0 * math.pi * (node + 0.5) / total
+        zr, zi = CENTRE + RADIUS * math.cos(theta), RADIUS * math.sin(theta)
+        wr, wi = RADIUS * math.cos(theta) / total, RADIUS * math.sin(theta) / total
+        decay = math.exp(-zr)
+        nodes.append(
+            dict(
+                zr=zr,
+                zi=zi,
+                er=decay * math.cos(zi),
+                ei=decay * math.sin(zi),
+                first=(2.0 * wr, 2.0 * wi),
+                second=(2.0 * (wr * zr - wi * zi), 2.0 * (wr * zi + wi * zr)),
+            )
+        )
+    return nodes
+
+
+def kernel(
+    nodes,
+    groups,
+    doms,
+    planes,
+    ny,
+    probes_ref,
+    slope_ref,
+    root_ref,
+    damping_ref,
+    moments_ref,
+    projections_ref,
+    coef,
+    rhs,
+    local,
+    basis,
+    q,
+    even,
+    odd,
+    outgoing,
+    incoming,
+    partial,
+    gathered,
+    shared,
+    own_sem,
+    field_send,
+    field_recv,
+    term_send,
+    term_recv,
+    dom_send,
+    dom_recv,
+    node_send,
+    node_recv,
+    out_sem,
+):
+    g = lax.axis_index("node")
+    d = lax.axis_index("dom")
+    rows = planes * ny
+    half = len(nodes)
+    nx = doms * planes
+    nz = rhs.shape[-1]
+    fields = (slope_ref, root_ref, damping_ref)
+
+    barrier = pltpu.get_barrier_semaphore()
+    for r in range(1, doms):
+        pl.semaphore_signal(barrier, inc=1, device_id={"dom": d ^ r}, device_id_type=MESH)
+    for s in range(1, groups):
+        pl.semaphore_signal(
+            barrier, inc=1, device_id={"node": lax.rem(g + s, groups)}, device_id_type=MESH
+        )
+
+    mine = pl.ds(pl.multiple_of(d * rows, rows), rows)
+    own = [pltpu.make_async_copy(f, coef.at[i, mine], own_sem.at[i]) for i, f in enumerate(fields)]
+    own.append(
+        pltpu.make_async_copy(
+            probes_ref.at[pl.ds((g * doms + d) * rows, rows)], rhs.at[mine], own_sem.at[3]
+        )
+    )
+    whole_local = pltpu.make_async_copy(probes_ref, local, own_sem.at[4])
+    for copy in own:
+        copy.start()
+    whole_local.start()
+    pl.semaphore_wait(barrier, doms - 1 + groups - 1)
+
+    sends = {}
+    for r in range(doms - 1, 0, -1):
+        e = d ^ r
+        pieces = []
+        for i, f in enumerate(fields):
+            pieces.append((f, coef.at[i, mine]))
+        pieces.append((probes_ref.at[pl.ds((g * doms + e) * rows, rows)], rhs.at[mine]))
+        for i, (src, dst) in enumerate(pieces):
+            copy = pltpu.make_async_remote_copy(
+                src_ref=src,
+                dst_ref=dst,
+                send_sem=field_send.at[r, i],
+                recv_sem=field_recv.at[r, i],
+                device_id={"dom": e},
+                device_id_type=MESH,
+            )
+            copy.start()
+            sends[r, i] = copy
+
+    blank = jnp.zeros((2, 8, nz), jnp.float32)
+    for buffer in (even, odd):
+        for k in range(half):
+            for end in (0, nx + 1):
+                buffer[k, :, end] = jnp.zeros((2, ny + 16, nz), jnp.float32)
+
+            def clear(x, _, buffer=buffer, k=k):
+                buffer[k, :, x, 0:8] = blank
+                buffer[k, :, x, ny + 8 : ny + 16] = blank
+                return 0
+
+            lax.fori_loop(1, nx + 1, clear, 0)
+    partial[...] = jnp.zeros(partial.shape, jnp.float32)
+
+    lane = lax.broadcasted_iota(jnp.int32, (ny, nz), 1)
+    first_lane, last_lane = lane == 0, lane == nz - 1
+
+    def start_plane(x):
+        at = pl.ds(pl.multiple_of(x * ny, ny), ny)
+        slope, root, damping = coef[0, at], coef[1, at], coef[2, at]
+        b = rhs[at]
+        for k, c in enumerate(nodes):
+            re = slope * (c["zr"] - root) + damping * c["er"]
+            im = slope * c["zi"] - damping * c["ei"]
+            scale = 1.0 / (re * re + im * im)
+            re = re * scale
+            im = -im * scale
+            q[k, 0, at] = re
+            q[k, 1, at] = im
+            even[k, 0, x + 1, 8 : ny + 8] = b * re
+            even[k, 1, x + 1, 8 : ny + 8] = b * im
+
+    for copy in own:
+        copy.wait()
+    for p in range(planes):
+        start_plane(d * planes + p)
+
+    whole_local.wait()
+    vectors = local.shape[0] // rows
+    for t in range(rows):
+        values = local[pl.ds(t, vectors, stride=rows), :]
+        high = values.astype(jnp.bfloat16)
+        low = (values - high.astype(jnp.float32)).astype(jnp.bfloat16)
+        basis[0, :, t * nz : (t + 1) * nz] = high
+        basis[1, :, t * nz : (t + 1) * nz] = low
+
+    for r in range(1, doms):
+        for i in range(4):
+            sends[r, i].wait_recv()
+        for p in range(planes):
+            start_plane((d ^ r) * planes + p)
+
+    def neighbours(source, k, c, x):
+        centre = source[k, c, x + 1, 8 : ny + 8]
+        total = source[k, c, x, 8 : ny + 8] + source[k, c, x + 2, 8 : ny + 8]
+        total = total + (source[k, c, x + 1, 7 : ny + 7] + source[k, c, x + 1, 9 : ny + 9])
+        before = jnp.where(first_lane, 0.0, pltpu.roll(centre, 1, 1))
+        after = jnp.where(last_lane, 0.0, pltpu.roll(centre, nz - 1, 1))
+        return total + (before + after)
+
+    def update(source, k, x, b):
+        at = pl.ds(pl.multiple_of(x * ny, ny), ny)
+        re = b + neighbours(source, k, 0, x)
+        im = neighbours(source, k, 1, x)
+        qre, qim = q[k, 0, at], q[k, 1, at]
+        return re * qre - im * qim, re * qim + im * qre
+
+    def sweep(source, target):
+        def step(i, _):
+            for u in range(UNROLL):
+                x = i * UNROLL + u
+                b = rhs[pl.ds(pl.multiple_of(x * ny, ny), ny)]
+                for k in range(half):
+                    re, im = update(source, k, x, b)
+                    target[k, 0, x + 1, 8 : ny + 8] = re
+                    target[k, 1, x + 1, 8 : ny + 8] = im
+            return 0
+
+        lax.fori_loop(0, nx // UNROLL, step, 0)
+
+    def pair(_, carry):
+        sweep(even, odd)
+        sweep(odd, even)
+        return carry
+
+    lax.fori_loop(0, (SWEEPS - 1) // 2, pair, 0)
+    source = even
+    if (SWEEPS - 1) % 2:
+        sweep(even, odd)
+        source = odd
+
+    backs = {}
+
+    def send_terms(r):
+        copy = pltpu.make_async_remote_copy(
+            src_ref=outgoing.at[r],
+            dst_ref=incoming.at[:, mine],
+            send_sem=term_send.at[r],
+            recv_sem=term_recv.at[r],
+            device_id={"dom": d ^ r},
+            device_id_type=MESH,
+        )
+        copy.start()
+        backs[r] = copy
+
+    for r in range(doms - 1, -1, -1):
+        for p in range(planes):
+            x = (d ^ r) * planes + p
+            b = rhs[pl.ds(pl.multiple_of(x * ny, ny), ny)]
+            first = second = None
+            for k, c in enumerate(nodes):
+                re, im = update(source, k, x, b)
+                one = re * c["first"][0] - im * c["first"][1]
+                two = re * c["second"][0] - im * c["second"][1]
+                first = one if first is None else first + one
+                second = two if second is None else second + two
+            if r:
+                outgoing[r, 0, p * ny : (p + 1) * ny] = first
+                outgoing[r, 1, p * ny : (p + 1) * ny] = second
+            else:
+                at = pl.ds(pl.multiple_of(d * rows + p * ny, ny), ny)
+                incoming[0, at] = first
+                incoming[1, at] = second
+        if r + 1 < doms:
+            send_terms(r + 1)
+
+    for r in range(doms - 1, 0, -1):
+        backs[r].wait_recv()
+    result = pltpu.make_async_copy(incoming, moments_ref, out_sem)
+    result.start()
+
+    highs, lows = [], []
+    for t in range(rows):
+        values = jnp.concatenate(
+            [incoming[m, pl.ds(t, doms, stride=rows), :] for m in range(2)], axis=0
+        )
+        high = values.astype(jnp.bfloat16)
+        highs.append(high)
+        lows.append((values - high.astype(jnp.float32)).astype(jnp.bfloat16))
+    left = jnp.concatenate([jnp.concatenate(highs, axis=1), jnp.concatenate(lows, axis=1)], axis=0)
+    dims = (((1,), (1,)), ((), ()))
+    product = lax.dot_general(
+        left, basis[0], dims, preferred_element_type=jnp.float32
+    ) + lax.dot_general(left, basis[1], dims, preferred_element_type=jnp.float32)
+    product = (product[: 2 * doms] + product[2 * doms :]) * (1.0 / (nx * ny * nz))
+    partial[:, :vectors] = product
+    gathered[d] = partial[...]
+
+    copies = []
+    for r in range(doms - 1, 0, -1):
+        copy = pltpu.make_async_remote_copy(
+            src_ref=partial,
+            dst_ref=gathered.at[d],
+            send_sem=dom_send.at[r],
+            recv_sem=dom_recv.at[r],
+            device_id={"dom": d ^ r},
+            device_id_type=MESH,
+        )
+        copy.start()
+        copies.append(copy)
+    for copy in copies:
+        copy.wait_recv()
+    total = gathered[0]
+    for e in range(1, doms):
+        total = total + gathered[e]
+    shared[g] = total
+    spread = []
+    for s in range(1, groups):
+        copy = pltpu.make_async_remote_copy(
+            src_ref=shared.at[g],
+            dst_ref=shared.at[g],
+            send_sem=node_send.at[s],
+            recv_sem=node_recv.at[s],
+            device_id={"node": lax.rem(g + s, groups)},
+            device_id_type=MESH,
+        )
+        copy.start()
+        spread.append(copy)
+    for r in range(1, doms):
+        for i in range(4):
+            sends[r, i].wait_send()
+        backs[r].wait_send()
+    for copy in copies:
+        copy.wait_send()
+    for copy in spread:
+        copy.wait()
+    for n in range(groups):
+        for m in range(2):
+            projections_ref[m, n * doms : (n + 1) * doms, :] = shared[n, m * doms : (m + 1) * doms, :vectors]
+    result.wait()
+
+
+def fused(total, groups, doms, probes, slope, root, damping):
+    vectors, planes, ny, nz = probes.shape
+    rows, nx, half = planes * ny, planes * doms, total // 2
+    anywhere = pl.BlockSpec(memory_space=pl.ANY)
+    grid = (half, 2, nx + 2, ny + 16, nz)
+    moments, projections = pl.pallas_call(
+        functools.partial(kernel, contour(total), groups, doms, planes, ny),
+        out_shape=(
+            jax.ShapeDtypeStruct((2, doms * rows, nz), jnp.float32),
+            jax.ShapeDtypeStruct((2, vectors, vectors), jnp.float32),
+        ),
+        in_specs=[anywhere] * 4,
+        out_specs=(anywhere, pl.BlockSpec(memory_space=pltpu.VMEM)),
+        scratch_shapes=[
+            pltpu.VMEM((3, nx * ny, nz), jnp.float32),
+            pltpu.VMEM((nx * ny, nz), jnp.float32),
+            pltpu.VMEM((vectors * rows, nz), jnp.float32),
+            pltpu.VMEM((2, vectors, rows * nz), jnp.bfloat16),
+            pltpu.VMEM((half, 2, nx * ny, nz), jnp.float32),
+            pltpu.VMEM(grid, jnp.float32),
+            pltpu.VMEM(grid, jnp.float32),
+            pltpu.VMEM((doms, 2, rows, nz), jnp.float32),
+            pltpu.VMEM((2, doms * rows, nz), jnp.float32),
+            pltpu.VMEM((2 * doms, 128), jnp.float32),
+            pltpu.VMEM((doms, 2 * doms, 128), jnp.float32),
+            pltpu.VMEM((groups, 2 * doms, 128), jnp.float32),
+            pltpu.SemaphoreType.DMA((5,)),
+            pltpu.SemaphoreType.DMA((doms, 4)),
+            pltpu.SemaphoreType.DMA((doms, 4)),
+            pltpu.SemaphoreType.DMA((doms,)),
+            pltpu.SemaphoreType.DMA((doms,)),
+            pltpu.SemaphoreType.DMA((doms,)),
+            pltpu.SemaphoreType.DMA((doms,)),
+            pltpu.SemaphoreType.DMA((groups,)),
+            pltpu.SemaphoreType.DMA((groups,)),
+            pltpu.SemaphoreType.DMA,
+        ],
+        compiler_params=pltpu.CompilerParams(collective_id=0, has_side_effects=True),
+    )(
+        probes.reshape(vectors * rows, nz),
+        slope.reshape(rows, nz),
+        root.reshape(rows, nz),
+        damping.reshape(rows, nz),
+    )
+    moments = moments.reshape(2, 1, doms, planes, ny, nz)
+    moments = jnp.pad(moments, ((0, 0), (0, 1)) + ((0, 0),) * 4)
+    projections = jnp.pad(projections[:, None], ((0, 0), (0, 1), (0, 0), (0, 0)))
+    return moments, projections
+
+
 def solution(mesh):
+    groups, doms = mesh.shape["node"], mesh.shape["dom"]
+
+    def step(probes, slope, root, damping):
+        vectors, ny = probes.shape[0], probes.shape[2]
+        one_each = vectors == groups * doms and doms & (doms - 1) == 0 and doms % 8 == 0
+        if one_each and ny % 8 == 0 and vectors <= 128 and probes.shape[3] % 128 == 0:
+            return fused(NODE_DEV * groups, groups, doms, probes, slope, root, damping)
+        return body(probes, slope, root, damping)
+
     in_specs = (
         P(None, "dom", None, None),
         P("dom", None, None),
@@ -111,4 +472,4 @@
         P("dom", None, None),
     )
     out_specs = (P(None, None, "node", "dom", None, None), P())
-    return jax.shard_map(body, mesh=mesh, in_specs=in_specs, out_specs=out_specs, check_vma=False)
+    return jax.shard_map(step, mesh=mesh, in_specs=in_specs, out_specs=out_specs, check_vma=False)

time: 261 us -> 38.3 us (0.15)
  blocking collectives: 131 us -> 0 us
  other arithmetic: 54.8 us -> 0 us
  waiting for transfers between devices: 46.8 us -> 0 us
  Pallas kernels: 0 us -> 35 us
  between operations: 14.3 us -> 0.65 us
  starting transfers between devices: 5.24 us -> 0 us
  local copies, waits for them, and re-layouts: 5.8 us -> 2.45 us
  matrix products: 3.08 us -> 0 us
    all_to_all x1 -> x0, blocking collectives: 51.6 us -> none  [body(): back = lax.all_to_all(terms, 'dom', split_axis=3, concat_axis=2, tiled=True)]
    psum x1 -> x0, waiting for transfers between devices: 46.1 us -> none  [body(): summed = lax.psum(local, 'node')]
    psum x1 -> x0, blocking collectives: 42.9 us -> none  [body(): lax.psum(partial_value.reshape(2, 2, vectors, vectors) / cells, ('node',...]
    all_gather x3 -> x0, blocking collectives: 36.2 us -> none  [the longest x1 18.8 us: body(): lax.all_gather(slope, 'dom', axis=0, tiled=True)]
    pallas_call x0 -> x1, Pallas kernels: none -> 35 us  [fused(): pl.pallas_call(functools.partial(kernel, contour(total), groups, doms, pl...]
    add x9 -> x0, other arithmetic: 26.4 us -> none  [the longest x8 26.4 us: grid_step(): total = total + padded[:, :, 1:-1, 1:-1, 2:] + padded[:, :, 1:-1, 1:-1, :-2]]
    another operation x10 -> x0, other arithmetic: 20.3 us -> none  [the longest x7 16.9 us: grid_step(): jnp.stack([real_part * factor_re - imag_part * factor_im, real_part * fac...]
    sub x10 -> x0, other arithmetic: 6.96 us -> none  [the longest x7 5.49 us: grid_step(): real_part * factor_re - imag_part * factor_im]
  transfers between devices with their start and end apart: 2 -> 0, of which waited for: 1 -> 0; matrix products, arithmetic and copies ran while one was open for 0% -> 0% of each run, Pallas kernels for 0% -> 0%
where the time goes in v1:
time: 38.3 us; the launch traced here: 38.1 us
  Pallas kernels  35 us (91%)
  local copies, waits for them, and re-layouts  2.45 us (6%)
  between operations  0.65 us (2%)
    pallas_call x1, Pallas kernels, fused(): pl.pallas_call(functools.partial(kernel, contour(total), groups, doms, pl...  35 us
    pad x1, local copies, waits for them, and re-layouts, fused(): moments = jnp.pad(moments, ((0, 0), (0, 1)) + ((0, 0),) * 4)  1.81 us

profile of v1, /device:TPU:0, one launch (start us, length us, event | category | flops | bytes accessed | tf_op | source)
XLA Modules:
  0.0 38.1 jit_solution(11585227425825100101)
XLA Ops:
  0.6 35.0 %shard_map.59 = (f32[2,256,128]{2,1,0:T(8,128)}, f32[2,32,32]{2,1,0:T(8,128)}) custom-call(f32[1024,128]{1,0:T(8,128)} %bitcast.10, f32[32,128]{1,0:T(8,128)} %bitcast.13, f32[32,128]{1,0:T(8,128)} %bitcast.14, f32[32,128]{1,0:T(8,128)} %bitcast.15), custom_call_target="tpu_custom_call" | custom-call | tf_op jit(solution)/shard_map/pallas_call | solution.py:413
  35.7 0.0 copy-start
  35.7 1.8 %pad.8 = f32[2,2,8,2,16,128]{5,4,3,2,1,0:T(8,128)} pad(f32[2,1,8,2,16,128]{5,4,3,2,1,0:T(8,128)} %bitcast.11, f32[]{:T(128)} %constant.2.clone.1), padding=0_0x0_1x0_0x0_0x0_0x0_0 | pad | bytes 786436 | tf_op jit(solution)/shard_map/jit(_pad)/pad | solution.py:453
  37.5 0.0 copy-done
  37.5 0.6 %pad.9.clone = f32[2,2,32,32]{3,2,1,0:T(8,128)} pad(f32[2,1,32,32]{3,2,1,0:T(8,128)S(1)} %bitcast.12, f32[]{:T(128)} %constant.2.clone.1), padding=0_0x0_1x0_0x0_0 | pad | bytes 24580 | tf_op jit(solution)/shard_map/jit(_pad)/pad | solution.py:454
Async XLA Ops:
  35.7 1.8 %copy-start = (f32[2,32,32]{2,1,0:T(8,128)S(1)}, f32[2,32,32]{2,1,0:T(8,128)}, u32[]{:S(2)}) copy-start(f32[2,32,32]{2,1,0:T(8,128)} %get-tuple-element.5) | copy-start | bytes 24580

commit v2 on v1

--- a/solution.py
+++ b/solution.py
@@ -10,7 +10,7 @@
 
 NODE_DEV = 2
 SWEEPS = 8
-UNROLL = 2
+UNROLL = 16
 
 
 CENTRE = 0.5

time: 38.3 us -> 34.6 us (0.903)
  Pallas kernels: 35 us -> 31.3 us
    pallas_call x1, Pallas kernels: 35 us -> 31.3 us  [fused(): pl.pallas_call(functools.partial(kernel, contour(total), groups, doms, pl...]
where the time goes in v2:
time: 34.6 us; the launch traced here: 34.4 us
  Pallas kernels  31.3 us (90%)
  local copies, waits for them, and re-layouts  2.45 us (7%)
  between operations  0.65 us (2%)
    pallas_call x1, Pallas kernels, fused(): pl.pallas_call(functools.partial(kernel, contour(total), groups, doms, pl...  31.3 us
    pad x1, local copies, waits for them, and re-layouts, fused(): moments = jnp.pad(moments, ((0, 0), (0, 1)) + ((0, 0),) * 4)  1.81 us

profile of v2, /device:TPU:0, one launch (start us, length us, event | category | flops | bytes accessed | tf_op | source)
XLA Modules:
  0.0 34.4 jit_solution(18208039953174268389)
XLA Ops:
  0.6 31.3 %shard_map.59 = (f32[2,256,128]{2,1,0:T(8,128)}, f32[2,32,32]{2,1,0:T(8,128)}) custom-call(f32[1024,128]{1,0:T(8,128)} %bitcast.10, f32[32,128]{1,0:T(8,128)} %bitcast.13, f32[32,128]{1,0:T(8,128)} %bitcast.14, f32[32,128]{1,0:T(8,128)} %bitcast.15), custom_call_target="tpu_custom_call" | custom-call | tf_op jit(solution)/shard_map/pallas_call | solution.py:413
  31.9 0.0 copy-start
  32.0 1.8 %pad.8 = f32[2,2,8,2,16,128]{5,4,3,2,1,0:T(8,128)} pad(f32[2,1,8,2,16,128]{5,4,3,2,1,0:T(8,128)} %bitcast.11, f32[]{:T(128)} %constant.2.clone.1), padding=0_0x0_1x0_0x0_0x0_0x0_0 | pad | bytes 786436 | tf_op jit(solution)/shard_map/jit(_pad)/pad | solution.py:453
  33.8 0.0 copy-done
  33.8 0.6 %pad.9.clone = f32[2,2,32,32]{3,2,1,0:T(8,128)} pad(f32[2,1,32,32]{3,2,1,0:T(8,128)S(1)} %bitcast.12, f32[]{:T(128)} %constant.2.clone.1), padding=0_0x0_1x0_0x0_0 | pad | bytes 24580 | tf_op jit(solution)/shard_map/jit(_pad)/pad | solution.py:454
Async XLA Ops:
  31.9 1.8 %copy-start = (f32[2,32,32]{2,1,0:T(8,128)S(1)}, f32[2,32,32]{2,1,0:T(8,128)}, u32[]{:S(2)}) copy-start(f32[2,32,32]{2,1,0:T(8,128)} %get-tuple-element.5) | copy-start | bytes 24580

commit v3 on v2

--- a/solution.py
+++ b/solution.py
@@ -153,14 +153,11 @@
     incoming,
     partial,
     gathered,
-    shared,
     own_sem,
     field_send,
     field_recv,
     term_send,
     term_recv,
-    dom_send,
-    dom_recv,
     node_send,
     node_recv,
     out_sem,
@@ -195,23 +192,25 @@
     pl.semaphore_wait(barrier, doms - 1 + groups - 1)
 
     sends = {}
+
+    def send_field(r, i, src, dst):
+        copy = pltpu.make_async_remote_copy(
+            src_ref=src,
+            dst_ref=dst,
+            send_sem=field_send.at[r, i],
+            recv_sem=field_recv.at[r, i],
+            device_id={"dom": d ^ r},
+            device_id_type=MESH,
+        )
+        copy.start()
+        sends[r, i] = copy
+
+    for r in list(range(doms - 2, 0, -2)) + [1]:
+        for i, f in enumerate(fields):
+            send_field(r, i, f, coef.at[i, mine])
     for r in range(doms - 1, 0, -1):
-        e = d ^ r
-        pieces = []
-        for i, f in enumerate(fields):
-            pieces.append((f, coef.at[i, mine]))
-        pieces.append((probes_ref.at[pl.ds((g * doms + e) * rows, rows)], rhs.at[mine]))
-        for i, (src, dst) in enumerate(pieces):
-            copy = pltpu.make_async_remote_copy(
-                src_ref=src,
-                dst_ref=dst,
-                send_sem=field_send.at[r, i],
-                recv_sem=field_recv.at[r, i],
-                device_id={"dom": e},
-                device_id_type=MESH,
-            )
-            copy.start()
-            sends[r, i] = copy
+        source = probes_ref.at[pl.ds((g * doms + (d ^ r)) * rows, rows)]
+        send_field(r, 3, source, rhs.at[mine])
 
     blank = jnp.zeros((2, 8, nz), jnp.float32)
     for buffer in (even, odd):
@@ -225,7 +224,6 @@
                 return 0
 
             lax.fori_loop(1, nx + 1, clear, 0)
-    partial[...] = jnp.zeros(partial.shape, jnp.float32)
 
     lane = lax.broadcasted_iota(jnp.int32, (ny, nz), 1)
     first_lane, last_lane = lane == 0, lane == nz - 1
@@ -259,9 +257,29 @@
         basis[0, :, t * nz : (t + 1) * nz] = high
         basis[1, :, t * nz : (t + 1) * nz] = low
 
-    for r in range(1, doms):
-        for i in range(4):
+    relays = {}
+    for r in range(2, doms, 2):
+        at = pl.ds(pl.multiple_of((d ^ r) * rows, rows), rows)
+        for i in range(3):
             sends[r, i].wait_recv()
+            copy = pltpu.make_async_remote_copy(
+                src_ref=coef.at[i, at],
+                dst_ref=coef.at[i, at],
+                send_sem=field_send.at[r + 1, i],
+                recv_sem=field_recv.at[r + 1, i],
+                device_id={"dom": d ^ 1},
+                device_id_type=MESH,
+            )
+            copy.start()
+            relays[r + 1, i] = copy
+    for r in [1] + list(range(2, doms, 2)) + list(range(3, doms, 2)):
+        if r == 1:
+            for i in range(3):
+                sends[r, i].wait_recv()
+        elif r % 2:
+            for i in range(3):
+                relays[r, i].wait_recv()
+        sends[r, 3].wait_recv()
         for p in range(planes):
             start_plane((d ^ r) * planes + p)
 
@@ -281,9 +299,11 @@
         return re * qre - im * qim, re * qim + im * qre
 
     def sweep(source, target):
+        unroll = math.gcd(UNROLL, nx)
+
         def step(i, _):
-            for u in range(UNROLL):
-                x = i * UNROLL + u
+            for u in range(unroll):
+                x = i * unroll + u
                 b = rhs[pl.ds(pl.multiple_of(x * ny, ny), ny)]
                 for k in range(half):
                     re, im = update(source, k, x, b)
@@ -291,7 +311,7 @@
                     target[k, 1, x + 1, 8 : ny + 8] = im
             return 0
 
-        lax.fori_loop(0, nx // UNROLL, step, 0)
+        lax.fori_loop(0, nx // unroll, step, 0)
 
     def pair(_, carry):
         sweep(even, odd)
@@ -358,50 +378,39 @@
         left, basis[0], dims, preferred_element_type=jnp.float32
     ) + lax.dot_general(left, basis[1], dims, preferred_element_type=jnp.float32)
     product = (product[: 2 * doms] + product[2 * doms :]) * (1.0 / (nx * ny * nz))
-    partial[:, :vectors] = product
-    gathered[d] = partial[...]
+    packs = partial.shape[1] // vectors
+    height = 2 * doms // packs
+    for n in range(packs):
+        partial[:, n * vectors : (n + 1) * vectors] = product[n * height : (n + 1) * height]
+    gathered[g, d] = partial[...]
 
     copies = []
-    for r in range(doms - 1, 0, -1):
-        copy = pltpu.make_async_remote_copy(
-            src_ref=partial,
-            dst_ref=gathered.at[d],
-            send_sem=dom_send.at[r],
-            recv_sem=dom_recv.at[r],
-            device_id={"dom": d ^ r},
-            device_id_type=MESH,
-        )
-        copy.start()
-        copies.append(copy)
+    for s in [*range(groups // 2, 0, -1), *range(groups // 2 + 1, groups), 0]:
+        for r in range(doms - 1, -1, -1):
+            if s or r:
+                copy = pltpu.make_async_remote_copy(
+                    src_ref=partial,
+                    dst_ref=gathered.at[g, d],
+                    send_sem=node_send.at[s, r],
+                    recv_sem=node_recv.at[s, r],
+                    device_id={"node": lax.rem(g + s, groups), "dom": d ^ r},
+                    device_id_type=MESH,
+                )
+                copy.start()
+                copies.append(copy)
+    for r in range(1, doms):
+        backs[r].wait_send()
+    for copy in list(sends.values()) + list(relays.values()):
+        copy.wait_send()
     for copy in copies:
-        copy.wait_recv()
-    total = gathered[0]
-    for e in range(1, doms):
-        total = total + gathered[e]
-    shared[g] = total
-    spread = []
-    for s in range(1, groups):
-        copy = pltpu.make_async_remote_copy(
-            src_ref=shared.at[g],
-            dst_ref=shared.at[g],
-            send_sem=node_send.at[s],
-            recv_sem=node_recv.at[s],
-            device_id={"node": lax.rem(g + s, groups)},
-            device_id_type=MESH,
-        )
-        copy.start()
-        spread.append(copy)
-    for r in range(1, doms):
-        for i in range(4):
-            sends[r, i].wait_send()
-        backs[r].wait_send()
-    for copy in copies:
-        copy.wait_send()
-    for copy in spread:
         copy.wait()
     for n in range(groups):
-        for m in range(2):
-            projections_ref[m, n * doms : (n + 1) * doms, :] = shared[n, m * doms : (m + 1) * doms, :vectors]
+        total = gathered[n, 0]
+        for e in range(1, doms):
+            total = total + gathered[n, e]
+        for k in range(packs):
+            m, j = divmod(k * height, doms)
+            projections_ref[m, n * doms + j : n * doms + j + height, :] = total[:, k * vectors : (k + 1) * vectors]
     result.wait()
 
 
@@ -428,18 +437,15 @@
             pltpu.VMEM(grid, jnp.float32),
             pltpu.VMEM((doms, 2, rows, nz), jnp.float32),
             pltpu.VMEM((2, doms * rows, nz), jnp.float32),
-            pltpu.VMEM((2 * doms, 128), jnp.float32),
-            pltpu.VMEM((doms, 2 * doms, 128), jnp.float32),
-            pltpu.VMEM((groups, 2 * doms, 128), jnp.float32),
+            pltpu.VMEM((2 * doms * vectors // 128, 128), jnp.float32),
+            pltpu.VMEM((groups, doms, 2 * doms * vectors // 128, 128), jnp.float32),
             pltpu.SemaphoreType.DMA((5,)),
             pltpu.SemaphoreType.DMA((doms, 4)),
             pltpu.SemaphoreType.DMA((doms, 4)),
             pltpu.SemaphoreType.DMA((doms,)),
             pltpu.SemaphoreType.DMA((doms,)),
-            pltpu.SemaphoreType.DMA((doms,)),
-            pltpu.SemaphoreType.DMA((doms,)),
-            pltpu.SemaphoreType.DMA((groups,)),
-            pltpu.SemaphoreType.DMA((groups,)),
+            pltpu.SemaphoreType.DMA((groups, doms)),
+            pltpu.SemaphoreType.DMA((groups, doms)),
             pltpu.SemaphoreType.DMA,
         ],
         compiler_params=pltpu.CompilerParams(collective_id=0, has_side_effects=True),
@@ -461,7 +467,7 @@
     def step(probes, slope, root, damping):
         vectors, ny = probes.shape[0], probes.shape[2]
         one_each = vectors == groups * doms and doms & (doms - 1) == 0 and doms % 8 == 0
-        if one_each and ny % 8 == 0 and vectors <= 128 and probes.shape[3] % 128 == 0:
+        if one_each and ny % 8 == 0 and 128 % vectors == 0 and probes.shape[3] % 128 == 0:
             return fused(NODE_DEV * groups, groups, doms, probes, slope, root, damping)
         return body(probes, slope, root, damping)
 

time: 34.6 us -> 31.1 us (0.90)
  Pallas kernels: 31.3 us -> 27.9 us
    pallas_call x1, Pallas kernels: 31.3 us -> 27.9 us  [fused(): pl.pallas_call(functools.partial(kernel, contour(total), groups, doms, pl...]
where the time goes in v3:
time: 31.1 us; the launch traced here: 31 us
  Pallas kernels  27.9 us (90%)
  local copies, waits for them, and re-layouts  2.45 us (8%)
  between operations  0.65 us (2%)
    pallas_call x1, Pallas kernels, fused(): pl.pallas_call(functools.partial(kernel, contour(total), groups, doms, pl...  27.9 us
    pad x1, local copies, waits for them, and re-layouts, fused(): moments = jnp.pad(moments, ((0, 0), (0, 1)) + ((0, 0),) * 4)  1.81 us
    pad x1, local copies, waits for them, and re-layouts, fused(): jnp.pad(projections[:, None], ((0, 0), (0, 1), (0, 0), (0, 0)))  0.63 us

profile of v3, /device:TPU:0, one launch (start us, length us, event | category | flops | bytes accessed | tf_op | source)
XLA Modules:
  0.0 31.0 jit_solution(13509547181148079753)
XLA Ops:
  0.6 27.9 %shard_map.59 = (f32[2,256,128]{2,1,0:T(8,128)}, f32[2,32,32]{2,1,0:T(8,128)}) custom-call(f32[1024,128]{1,0:T(8,128)} %bitcast.10, f32[32,128]{1,0:T(8,128)} %bitcast.13, f32[32,128]{1,0:T(8,128)} %bitcast.14, f32[32,128]{1,0:T(8,128)} %bitcast.15), custom_call_target="tpu_custom_call" | custom-call | tf_op jit(solution)/shard_map/pallas_call | solution.py:422
  28.5 0.0 copy-start
  28.5 1.8 %pad.8 = f32[2,2,8,2,16,128]{5,4,3,2,1,0:T(8,128)} pad(f32[2,1,8,2,16,128]{5,4,3,2,1,0:T(8,128)} %bitcast.11, f32[]{:T(128)} %constant.2.clone.1), padding=0_0x0_1x0_0x0_0x0_0x0_0 | pad | bytes 786436 | tf_op jit(solution)/shard_map/jit(_pad)/pad | solution.py:459
  30.4 0.0 copy-done
  30.4 0.6 %pad.9.clone = f32[2,2,32,32]{3,2,1,0:T(8,128)} pad(f32[2,1,32,32]{3,2,1,0:T(8,128)S(1)} %bitcast.12, f32[]{:T(128)} %constant.2.clone.1), padding=0_0x0_1x0_0x0_0 | pad | bytes 24580 | tf_op jit(solution)/shard_map/jit(_pad)/pad | solution.py:460
Async XLA Ops:
  28.5 1.8 %copy-start = (f32[2,32,32]{2,1,0:T(8,128)S(1)}, f32[2,32,32]{2,1,0:T(8,128)}, u32[]{:S(2)}) copy-start(f32[2,32,32]{2,1,0:T(8,128)} %get-tuple-element.5) | copy-start | bytes 24580
